TPU v7x, 32 devices: a whole 2x2x4 slice. The times are simulated.
32 devices in a mesh: dom: 16 (over z, y, x), orb: 2 (over core).
Axes of the slice: x: 2, y: 2, z: 4, core: 2. Of those that a mesh axis runs over, the one named last changes fastest.
Arguments:
- orbitals: bfloat16 [768, 64, 512], P('dom', 'orb'), may hold values from -6 to 6
- adjoint_source: bfloat16 [768, 64, 512], P('dom', 'orb'), may hold values from -6 to 6
- eigenvalues: float32 [64], P('orb'), may hold values from -1 to -0.25
- cell_scale: float32 [768], P('dom'), may hold values from 0.4 to 1.6
- base_potential: float32 [768, 512], P('dom'), may hold values from 0.5 to 1.5
- stiffness: bfloat16 [512, 512], replicated, may hold values from -1.5 to 1.5, as said below
- face_perm: int32 [768, 64], P('dom'), may hold values from 0 to 63, each once within a row
- restrict: bfloat16 [512, 64], replicated, may hold values from -0.25 to 0.25
- prolong: bfloat16 [64, 512], replicated, may hold values from -0.75 to 0.75
- owner: int32 [768, 1], P('dom'), may hold values from 0 to 15; in each aligned block of 48 rows (0 to 47, 48 to 95, ...) at most 6 rows name the same one
- pot_slot: int32 [768], P('dom'), may hold values from 0 to 63
- potential: float32 [1024, 64], P('dom'), may hold values from -6 to 6
Outputs:
- adjoint: bfloat16 [768, 64, 512], P('dom', 'orb')
- updated: float32 [1024, 64], P('dom')
- applied: bfloat16 [768, 64, 512], P('dom', 'orb')
Inputs may be any that keep to these rules, and one draw needn't show every extreme that they name: In the rows of one device no owner is named by more than 6 cells. `face_perm`: each row is a permutation. `stiffness`: symmetric.
All inputs are finite; a program needn't handle non-finite values.
Results may differ from a plain program's by a relative error of at most 0.0027.
Values sent between devices are 32-bit elements; how exact they have to be, the bound alone decides.
A program may use at most 64 MiB of HBM per device.

v0:
```python
import jax
import jax.numpy as jnp
from jax import lax
from jax.sharding import PartitionSpec as P

ITERS = 4
relax = 0.25
step_rate = 0.1


def padded_2(block, sides, width):
    for axis, dim in sides:
        count = lax.axis_size(axis)
        forward = [(i, i + 1) for i in range(count - 1)]
        backward = [(target, source) for source, target in forward]
        low = lax.ppermute(
            lax.slice_in_dim(block, block.shape[dim] - width, None, axis=dim), axis, forward
        )
        high = lax.ppermute(lax.slice_in_dim(block, 0, width, axis=dim), axis, backward)
        block = jnp.concatenate([low, block, high], axis=dim)
    return block


def local(
    orbitals,
    adjoint_source,
    eigenvalues,
    cell_scale,
    base_potential,
    stiffness,
    face_perm,
    restrict,
    prolong,
    owner,
    pot_slot,
    potential,
):
    nodes = stiffness.shape[0]
    faces = face_perm.shape[1]
    pot_rows = potential.shape[0]
    n_domains = lax.axis_size("dom")
    cell_count = owner.shape[0]
    capacity = 2 * ((cell_count + n_domains - 1) // n_domains)
    onehot = (face_perm[:, :, None] == jnp.arange(faces, dtype=jnp.int32)[None, None, :]).astype(
        jnp.float32
    )

    def assemble_local(partial_sum):
        left_face = partial_sum[:, :, :faces]
        right_face = partial_sum[:, :, nodes - faces :]
        sent_right = jnp.einsum("ckj,cok->coj", onehot, right_face, precision=lax.Precision.HIGHEST)
        boundary = jnp.stack([left_face[0], sent_right[-1]], 0)
        padded = padded_2(boundary, (("dom", 0),), 1)
        left_next = jnp.concatenate([left_face[1:], padded[3][None]], 0)
        add_right = jnp.einsum("ckj,coj->cok", onehot, left_next, precision=lax.Precision.HIGHEST)
        add_left = jnp.concatenate([padded[0][None], sent_right[:-1]], 0)
        return jnp.concatenate(
            [
                left_face + add_left,
                partial_sum[:, :, faces : nodes - faces],
                right_face + add_right,
            ],
            2,
        )

    def operator(values_bf, values_full, shift):
        kinetic = jnp.dot(
            values_bf.reshape(-1, nodes), stiffness, preferred_element_type=jnp.float32
        ).reshape(values_full.shape)
        return assemble_local(cell_scale[:, None, None] * kinetic + shift * values_full)

    source = adjoint_source.astype(jnp.float32)
    shift = base_potential[:, None, :] - eigenvalues[None, :, None]
    iterate = relax * source
    for step_index in range(ITERS):
        image = operator(iterate.astype(jnp.bfloat16), iterate, shift)
        iterate = iterate + relax * (source - image)
    adjoint = iterate.astype(jnp.bfloat16)
    partial_density = jnp.sum(orbitals.astype(jnp.float32) * iterate, axis=1)
    restrict_full = restrict.astype(jnp.float32)
    density_term = lax.psum(partial_density, "orb")
    projected = jnp.dot(density_term, restrict_full, precision=lax.Precision.HIGHEST)
    coarse_cols = projected.shape[1]
    dest_owner = owner[:, 0]
    owner_hot = (dest_owner[:, None] == jnp.arange(n_domains, dtype=jnp.int32)[None, :]).astype(
        jnp.int32
    )
    earlier = jnp.cumsum(owner_hot, axis=0) - owner_hot
    rank_within = jnp.sum(earlier * owner_hot, axis=1)
    slot_index = dest_owner * capacity + rank_within
    send_hot_int = (
        slot_index[None, :] == jnp.arange(n_domains * capacity, dtype=jnp.int32)[:, None]
    ).astype(jnp.int32)
    send_hot = send_hot_int.astype(jnp.float32)
    send_values = jnp.dot(send_hot, projected, precision=lax.Precision.HIGHEST).reshape(
        n_domains, capacity, coarse_cols
    )
    send_ids = (jnp.sum(send_hot_int * (pot_slot + 1)[None, :], axis=1) - 1).reshape(
        n_domains, capacity
    )
    recv_values, recv_ids = (
        lax.all_to_all(send_values, "dom", split_axis=0, concat_axis=0, tiled=True),
        lax.all_to_all(send_ids, "dom", split_axis=0, concat_axis=0, tiled=True),
    )
    recv_hot = (
        recv_ids.reshape(-1)[None, :] == jnp.arange(pot_rows, dtype=jnp.int32)[:, None]
    ).astype(jnp.float32)
    summed = jnp.dot(
        recv_hot, recv_values.reshape(-1, coarse_cols), precision=lax.Precision.HIGHEST
    )
    updated = potential - step_rate * summed
    back_values = jnp.dot(recv_hot.T, updated, precision=lax.Precision.HIGHEST).reshape(
        n_domains, capacity, coarse_cols
    )
    returned = lax.all_to_all(back_values, "dom", split_axis=0, concat_axis=0, tiled=True)
    cell_pot = jnp.dot(
        send_hot.T, returned.reshape(-1, coarse_cols), precision=lax.Precision.HIGHEST
    )
    node_potential = jnp.dot(cell_pot, prolong.astype(jnp.float32), precision=lax.Precision.HIGHEST)
    shift_new = (base_potential + node_potential)[:, None, :]
    applied = operator(orbitals, orbitals.astype(jnp.float32), shift_new).astype(jnp.bfloat16)
    return (adjoint, updated, applied)


def solution(mesh):
    in_specs = (
        P("dom", "orb", None),
        P("dom", "orb", None),
        P("orb"),
        P("dom"),
        P("dom", None),
        P(),
        P("dom", None),
        P(),
        P(),
        P("dom", None),
        P("dom"),
        P("dom", None),
    )
    out_specs = (P("dom", "orb", None), P("dom", None), P("dom", "orb", None))
    return jax.shard_map(local, mesh=mesh, in_specs=in_specs, out_specs=out_specs, check_vma=False)
```

profile of v0, /device:TPU:8, one launch (start us, length us, event | category | flops | bytes accessed | tf_op | source)
XLA Modules:
  0.0 149.7 jit_solution(11445277540518210424)
XLA Ops:
  8.2 3.2 %fusion.11 = f32[48,32,512]{2,1,0:T(8,128)S(1)} fusion(bf16[48,32,512]{2,1,0:T(8,128)(2,1)} %param.13, f32[32]{0:T(128)} %param.14, f32[48,512]{1,0:T(8,128)} %param.16, f32[48]{0:T(128)} %param.15, bf16[512,512]{1,0:T(8,128)(2,1)S(1)} %copy-done), kind=kOutput, calls=%fused_computation.22 | convolution fusion | flops 812384256 | bytes 5341504 | tf_op jit(solution)/shard_map/dot_general | solution.py:67
  11.4 4.2 %collective-permute-start.1 = (f32[1,32,64]{2,1,0:T(8,128)S(1)}, f32[1,32,64]{2,1,0:T(8,128)S(1)}, u32[]{:S(2)}, u32[]{:S(2)}) collective-permute-start(f32[1,32,64]{2,1,0:T(8,128)S(1)} %slice.157), channel_id=1, source_target_pairs={{2,0},{4,2},{6,4},{8,6},{10,8},{12,10},{14,12},{16,14},{18,16},{20... | collective-permute-start | bytes 24584 | tf_op jit(solution)/shard_map/ppermute | solution.py:19
  17.5 1.9 %collective-permute-start = (f32[1,32,64]{2,1,0:T(8,128)S(1)}, f32[1,32,64]{2,1,0:T(8,128)S(1)}, u32[]{:S(2)}, u32[]{:S(2)}) collective-permute-start(f32[1,32,64]{2,1,0:T(8,128)S(1)} %slice.153), channel_id=1, source_target_pairs={{0,2},{2,4},{4,6},{6,8},{8,10},{10,12},{12,14},{14,16},{16,18},{18... | collective-permute-start | bytes 24584 | tf_op jit(solution)/shard_map/ppermute | solution.py:16
  21.2 2.7 %slice.155 = f32[48,32,384]{2,1,0:T(8,128)S(1)} slice(f32[48,32,512]{2,1,0:T(8,128)} %copy-done.1), slice={[0:48], [0:32], [64:448]} | slice | bytes 4718592 | tf_op jit(solution)/shard_map/slice | solution.py:60
  25.6 2.8 %fusion.12 = f32[48,32,512]{2,1,0:T(8,128)S(1)} fusion(f32[32]{0:T(128)S(1)} %copy-done.13, f32[48,512]{1,0:T(8,128)S(1)} %copy-done.7, f32[48]{0:T(128)S(1)} %copy-done.14, f32[48,32,64]{2,1,0:T(8,128)S(1)} %fusion.30, f32[48,32,384]{2,1,0:T(8,128)S(1)} %slice.155, f32[48,32,64]{2,1,0:T(8,128)S(1)} %slice_add_fusion.4, ...), kind=kOutput, calls=%fused_computation.23 | convolution fusion | flops 820248576 | bytes 8487232 | tf_op jit(solution)/shard_map/dot_general | solution.py:67
  28.4 5.7 %collective-permute-start.3 = (f32[1,32,64]{2,1,0:T(8,128)S(1)}, f32[1,32,64]{2,1,0:T(8,128)S(1)}, u32[]{:S(2)}, u32[]{:S(2)}) collective-permute-start(f32[1,32,64]{2,1,0:T(8,128)S(1)} %slice.164), channel_id=1, source_target_pairs={{2,0},{4,2},{6,4},{8,6},{10,8},{12,10},{14,12},{16,14},{18,16},{20... | collective-permute-start | bytes 24584 | tf_op jit(solution)/shard_map/ppermute | solution.py:19
  40.2 4.0 %collective-permute-done.2 = f32[1,32,64]{2,1,0:T(8,128)S(1)} collective-permute-done((f32[1,32,64]{2,1,0:T(8,128)S(1)}, f32[1,32,64]{2,1,0:T(8,128)S(1)}, u32[]{:S(2)}, u32[]{:S(2)}) %collective-permute-start.2) | collective-permute-done | bytes 8224 | tf_op jit(solution)/shard_map/ppermute | solution.py:16
  44.4 2.8 %fusion.6 = f32[48,32,512]{2,1,0:T(8,128)S(1)} fusion(bf16[48,32,512]{2,1,0:T(8,128)(2,1)S(1)} %copy-done.3, f32[48,32,64]{2,1,0:T(8,128)S(1)} %fusion.31, f32[48,32,384]{2,1,0:T(8,128)S(1)} %slice.162, f32[48,32,64]{2,1,0:T(8,128)S(1)} %slice_add_fusion.3, f32[48,32,64]{2,1,0:T(8,128)S(1)} %fusion.30, f32[48,32,384]{2,1,0:T(8,128)S(1)} %slice.155, ...), kind=kLoop, calls=%fused_computation.17 | loop fusion | flops 9437184 | bytes 11010048 | tf_op jit(solution)/shard_map/add | solution.py:77
  48.4 2.1 %collective-permute-start.5 = (f32[1,32,64]{2,1,0:T(8,128)S(1)}, f32[1,32,64]{2,1,0:T(8,128)S(1)}, u32[]{:S(2)}, u32[]{:S(2)}) collective-permute-start(f32[1,32,64]{2,1,0:T(8,128)S(1)} %slice.171), channel_id=1, source_target_pairs={{2,0},{4,2},{6,4},{8,6},{10,8},{12,10},{14,12},{16,14},{18,16},{20... | collective-permute-start | bytes 24584 | tf_op jit(solution)/shard_map/ppermute | solution.py:19
  53.2 3.9 %collective-permute-start.4 = (f32[1,32,64]{2,1,0:T(8,128)S(1)}, f32[1,32,64]{2,1,0:T(8,128)S(1)}, u32[]{:S(2)}, u32[]{:S(2)}) collective-permute-start(f32[1,32,64]{2,1,0:T(8,128)S(1)} %slice.167), channel_id=1, source_target_pairs={{0,2},{2,4},{4,6},{6,8},{8,10},{10,12},{12,14},{14,16},{16,18},{18... | collective-permute-start | bytes 24584 | tf_op jit(solution)/shard_map/ppermute | solution.py:16
  58.6 2.0 %collective-permute-done.4 = f32[1,32,64]{2,1,0:T(8,128)S(1)} collective-permute-done((f32[1,32,64]{2,1,0:T(8,128)S(1)}, f32[1,32,64]{2,1,0:T(8,128)S(1)}, u32[]{:S(2)}, u32[]{:S(2)}) %collective-permute-start.4) | collective-permute-done | bytes 8224 | tf_op jit(solution)/shard_map/ppermute | solution.py:16
  60.8 2.5 %fusion.14 = f32[48,32,512]{2,1,0:T(8,128)S(1)} fusion(f32[32]{0:T(128)S(1)} %copy-done.13, f32[48,512]{1,0:T(8,128)S(1)} %copy-done.7, f32[48]{0:T(128)S(1)} %copy-done.14, bf16[512,512]{1,0:T(8,128)(2,1)S(1)} %copy-done, f32[48,32,512]{2,1,0:T(8,128)S(1)} %fusion.6, f32[48,32,64]{2,1,0:T(8,128)S(1)} %fusion.32, f32[48,32,384]{2,1,0:T(8,128)S(1)} %slice.169, ...), kind=kOutput, calls=%fused_computation.25 | convolution fusion | flops 818675712 | bytes 11632960 | tf_op jit(solution)/shard_map/dot_general | solution.py:67
  67.9 4.1 %collective-permute-start.6 = (f32[1,32,64]{2,1,0:T(8,128)S(1)}, f32[1,32,64]{2,1,0:T(8,128)S(1)}, u32[]{:S(2)}, u32[]{:S(2)}) collective-permute-start(f32[1,32,64]{2,1,0:T(8,128)S(1)} %slice.174), channel_id=1, source_target_pairs={{0,2},{2,4},{4,6},{6,8},{8,10},{10,12},{12,14},{14,16},{16,18},{18... | collective-permute-start | bytes 24584 | tf_op jit(solution)/shard_map/ppermute | solution.py:16
  73.4 2.0 %collective-permute-done.6 = f32[1,32,64]{2,1,0:T(8,128)S(1)} collective-permute-done((f32[1,32,64]{2,1,0:T(8,128)S(1)}, f32[1,32,64]{2,1,0:T(8,128)S(1)}, u32[]{:S(2)}, u32[]{:S(2)}) %collective-permute-start.6) | collective-permute-done | bytes 8224 | tf_op jit(solution)/shard_map/ppermute | solution.py:16
  75.6 4.5 %fusion.2 = (f32[48,512]{1,0:T(8,128)}, bf16[48,32,512]{2,1,0:T(8,128)(2,1)}) fusion(bf16[48,32,512]{2,1,0:T(8,128)(2,1)S(1)} %copy-done.5, f32[48,32,64]{2,1,0:T(8,128)S(1)} %fusion.33, f32[48,32,384]{2,1,0:T(8,128)S(1)} %slice.176, f32[48,32,64]{2,1,0:T(8,128)S(1)} %slice_add_fusion.1, f32[48,32,512]{2,1,0:T(8,128)S(1)} %fusion.6, ...), kind=kLoop, calls=%fused_computation.13 | loop fusion | flops 11771904 | bytes 14254080 | tf_op jit(solution)/shard_map/reduce_sum | solution.py:79
  80.9 5.5 %all-to-all-start = ((s32[16,1,6]{2,1,0:T(1,128)}), s32[16,1,6]{2,1,0:T(1,128)S(1)}, u32[]{:S(2)}, u32[]{:S(2)}) async-start(s32[16,1,6]{2,1,0:T(1,128)} %bitcast.2), calls=%async_computation | async-start | bytes 16384 | tf_op jit(solution)/shard_map/all_to_all | solution.py:103
  86.4 11.5 %all-reduce.2.cloned.1.call-done = f32[48,512]{1,0:T(8,128)} async-done(((f32[48,512]{1,0:T(8,128)}), f32[48,512]{1,0:T(8,128)}) %all-reduce.2.cloned.1.call-update) | async-done | bytes 98320 | tf_op jit(solution)/shard_map/psum | solution.py:81
  100.1 7.0 %all-to-all-start.1 = ((f32[16,1,384]{2,1,0:T(1,128)}), f32[16,1,384]{2,1,0:T(1,128)S(1)}, u32[]{:S(2)}, u32[]{:S(2)}) async-start(f32[16,1,384]{2,1,0:T(1,128)} %reshape.84), calls=%async_computation.1 | async-start | bytes 49152 | tf_op jit(solution)/shard_map/all_to_all | solution.py:102
  108.3 4.8 %all-to-all-done.1 = f32[16,1,384]{2,1,0:T(1,128)S(1)} async-done(((f32[16,1,384]{2,1,0:T(1,128)}), f32[16,1,384]{2,1,0:T(1,128)S(1)}, u32[]{:S(2)}, u32[]{:S(2)}) %all-to-all-start.1) | async-done | bytes 24608 | tf_op jit(solution)/shard_map/all_to_all | solution.py:102
  114.9 9.9 %all_to_all.16 = f32[16,1,384]{2,1,0:T(1,128)S(1)} all-to-all(f32[16,1,384]{2,1,0:T(1,128)S(1)} %reshape.86), channel_id=1, replica_groups=mesh['dom'=16,'orb'=2] {'dom'}, dimensions={0} | all-to-all | bytes 49152 | tf_op jit(solution)/shard_map/all_to_all | solution.py:115
  127.1 3.6 %collective-permute-start.9 = (f32[1,32,64]{2,1,0:T(8,128)S(1)}, f32[1,32,64]{2,1,0:T(8,128)S(1)}, u32[]{:S(2)}, u32[]{:S(2)}) collective-permute-start(f32[1,32,64]{2,1,0:T(8,128)S(1)} %slice.185), channel_id=1, source_target_pairs={{2,0},{4,2},{6,4},{8,6},{10,8},{12,10},{14,12},{16,14},{18,16},{20... | collective-permute-start | bytes 24584 | tf_op jit(solution)/shard_map/ppermute | solution.py:19
  133.2 2.5 %collective-permute-start.8 = (f32[1,32,64]{2,1,0:T(8,128)S(1)}, f32[1,32,64]{2,1,0:T(8,128)S(1)}, u32[]{:S(2)}, u32[]{:S(2)}) collective-permute-start(f32[1,32,64]{2,1,0:T(8,128)S(1)} %slice.181), channel_id=1, source_target_pairs={{0,2},{2,4},{4,6},{6,8},{8,10},{10,12},{12,14},{14,16},{16,18},{18... | collective-permute-start | bytes 24584 | tf_op jit(solution)/shard_map/ppermute | solution.py:16
  137.4 3.2 %collective-permute-done.8 = f32[1,32,64]{2,1,0:T(8,128)S(1)} collective-permute-done((f32[1,32,64]{2,1,0:T(8,128)S(1)}, f32[1,32,64]{2,1,0:T(8,128)S(1)}, u32[]{:S(2)}, u32[]{:S(2)}) %collective-permute-start.8) | collective-permute-done | bytes 8224 | tf_op jit(solution)/shard_map/ppermute | solution.py:16
  140.7 2.1 %pad_maximum_fusion = bf16[48,32,512]{2,1,0:T(8,128)(2,1)} fusion(bf16[48,32,64]{2,1,0:T(8,128)(2,1)S(1)} %fusion.35, bf16[48,32,384]{2,1,0:T(8,128)(2,1)S(1)} %slice.209, bf16[48,32,64]{2,1,0:T(8,128)(2,1)S(1)} %fusion.38), kind=kLoop, calls=%fused_computation.27 | loop fusion | flops 4718592 | bytes 3145728 | tf_op jit(solution)/shard_map/concatenate | solution.py:57
  (110 shorter events, 36.2 us)
Async XLA Ops:
  7.2 8.5 %copy-start.4 = (s32[48,64]{1,0:T(8,128)S(1)}, s32[48,64]{1,0:T(8,128)}, u32[]{:S(2)}) copy-start(s32[48,64]{1,0:T(8,128)} %param.18) | copy-start | bytes 36868
  7.2 12.2 %copy-start.12 = (s32[48]{0:T(128)S(1)}, s32[48]{0:T(128)}, u32[]{:S(2)}) copy-start(s32[48]{0:T(128)} %param.22) | copy-start | bytes 580
  7.2 12.3 %copy-start.11 = (s32[48,1]{0,1:T(1,128)S(1)}, s32[48,1]{0,1:T(1,128)}, u32[]{:S(2)}) copy-start(s32[48,1]{0,1:T(1,128)} %param.21) | copy-start | bytes 580
  7.2 90.7 %all-reduce.2.cloned.1.call-start = ((), (), s32[]{:S(2)}) async-start(), calls=%async_computation.3 | async-start | bytes 196608 | tf_op jit(solution)/shard_map/psum | solution.py:81
  11.4 4.3 %copy-start.1 = (f32[48,32,512]{2,1,0:T(8,128)}, f32[48,32,512]{2,1,0:T(8,128)S(1)}, u32[]{:S(2)}) copy-start(f32[48,32,512]{2,1,0:T(8,128)S(1)} %fusion.11) | copy-start | bytes 9437188
  11.4 12.5 %collective-permute-start.1 = (f32[1,32,64]{2,1,0:T(8,128)S(1)}, f32[1,32,64]{2,1,0:T(8,128)S(1)}, u32[]{:S(2)}, u32[]{:S(2)}) collective-permute-start(f32[1,32,64]{2,1,0:T(8,128)S(1)} %slice.157), channel_id=1, source_target_pairs={{2,0},{4,2},{6,4},{8,6},{10,8},{12,10},{14,12},{16,14},{18,16},{20... | collective-permute-start | bytes 24584 | tf_op jit(solution)/shard_map/ppermute | solution.py:19
  17.5 7.9 %collective-permute-start = (f32[1,32,64]{2,1,0:T(8,128)S(1)}, f32[1,32,64]{2,1,0:T(8,128)S(1)}, u32[]{:S(2)}, u32[]{:S(2)}) collective-permute-start(f32[1,32,64]{2,1,0:T(8,128)S(1)} %slice.153), channel_id=1, source_target_pairs={{0,2},{2,4},{4,6},{6,8},{8,10},{10,12},{12,14},{14,16},{16,18},{18... | collective-permute-start | bytes 24584 | tf_op jit(solution)/shard_map/ppermute | solution.py:16
  21.1 2.8 %copy-start.2 = (f32[48,32,512]{2,1,0:T(8,128)S(1)}, f32[48,32,512]{2,1,0:T(8,128)}, u32[]{:S(2)}) copy-start(f32[48,32,512]{2,1,0:T(8,128)} %copy-done.1) | copy-start | bytes 9437188
  23.9 1.7 %copy-start.3 = (bf16[48,32,512]{2,1,0:T(8,128)(2,1)S(1)}, bf16[48,32,512]{2,1,0:T(8,128)(2,1)}, u32[]{:S(2)}) copy-start(bf16[48,32,512]{2,1,0:T(8,128)(2,1)} %param.13) | copy-start | bytes 4718596
  28.4 10.3 %collective-permute-start.3 = (f32[1,32,64]{2,1,0:T(8,128)S(1)}, f32[1,32,64]{2,1,0:T(8,128)S(1)}, u32[]{:S(2)}, u32[]{:S(2)}) collective-permute-start(f32[1,32,64]{2,1,0:T(8,128)S(1)} %slice.164), channel_id=1, source_target_pairs={{2,0},{4,2},{6,4},{8,6},{10,8},{12,10},{14,12},{16,14},{18,16},{20... | collective-permute-start | bytes 24584 | tf_op jit(solution)/shard_map/ppermute | solution.py:19
  36.8 7.4 %collective-permute-start.2 = (f32[1,32,64]{2,1,0:T(8,128)S(1)}, f32[1,32,64]{2,1,0:T(8,128)S(1)}, u32[]{:S(2)}, u32[]{:S(2)}) collective-permute-start(f32[1,32,64]{2,1,0:T(8,128)S(1)} %slice.160), channel_id=1, source_target_pairs={{0,2},{2,4},{4,6},{6,8},{8,10},{10,12},{12,14},{14,16},{16,18},{18... | collective-permute-start | bytes 24584 | tf_op jit(solution)/shard_map/ppermute | solution.py:16
  48.4 8.7 %collective-permute-start.5 = (f32[1,32,64]{2,1,0:T(8,128)S(1)}, f32[1,32,64]{2,1,0:T(8,128)S(1)}, u32[]{:S(2)}, u32[]{:S(2)}) collective-permute-start(f32[1,32,64]{2,1,0:T(8,128)S(1)} %slice.171), channel_id=1, source_target_pairs={{2,0},{4,2},{6,4},{8,6},{10,8},{12,10},{14,12},{16,14},{18,16},{20... | collective-permute-start | bytes 24584 | tf_op jit(solution)/shard_map/ppermute | solution.py:19
  53.2 7.4 %collective-permute-start.4 = (f32[1,32,64]{2,1,0:T(8,128)S(1)}, f32[1,32,64]{2,1,0:T(8,128)S(1)}, u32[]{:S(2)}, u32[]{:S(2)}) collective-permute-start(f32[1,32,64]{2,1,0:T(8,128)S(1)} %slice.167), channel_id=1, source_target_pairs={{0,2},{2,4},{4,6},{6,8},{8,10},{10,12},{12,14},{14,16},{16,18},{18... | collective-permute-start | bytes 24584 | tf_op jit(solution)/shard_map/ppermute | solution.py:16
  63.2 8.7 %collective-permute-start.7 = (f32[1,32,64]{2,1,0:T(8,128)S(1)}, f32[1,32,64]{2,1,0:T(8,128)S(1)}, u32[]{:S(2)}, u32[]{:S(2)}) collective-permute-start(f32[1,32,64]{2,1,0:T(8,128)S(1)} %slice.178), channel_id=1, source_target_pairs={{2,0},{4,2},{6,4},{8,6},{10,8},{12,10},{14,12},{16,14},{18,16},{20... | collective-permute-start | bytes 24584 | tf_op jit(solution)/shard_map/ppermute | solution.py:19
  67.8 7.7 %copy-start.5 = (bf16[48,32,512]{2,1,0:T(8,128)(2,1)S(1)}, bf16[48,32,512]{2,1,0:T(8,128)(2,1)}, u32[]{:S(2)}) copy-start(bf16[48,32,512]{2,1,0:T(8,128)(2,1)} %param.12) | copy-start | bytes 4718596
  67.9 7.6 %collective-permute-start.6 = (f32[1,32,64]{2,1,0:T(8,128)S(1)}, f32[1,32,64]{2,1,0:T(8,128)S(1)}, u32[]{:S(2)}, u32[]{:S(2)}) collective-permute-start(f32[1,32,64]{2,1,0:T(8,128)S(1)} %slice.174), channel_id=1, source_target_pairs={{0,2},{2,4},{4,6},{6,8},{8,10},{10,12},{12,14},{14,16},{16,18},{18... | collective-permute-start | bytes 24584 | tf_op jit(solution)/shard_map/ppermute | solution.py:16
  75.6 22.4 %copy-start.8 = (bf16[512,64]{0,1:T(8,128)(2,1)S(1)}, bf16[512,64]{0,1:T(8,128)(2,1)}, u32[]{:S(2)}) copy-start(bf16[512,64]{0,1:T(8,128)(2,1)} %param.19) | copy-start | bytes 196612
  75.6 38.8 %copy-start.10 = (f32[64,64]{1,0:T(8,128)S(1)}, f32[64,64]{1,0:T(8,128)}, u32[]{:S(2)}) copy-start(f32[64,64]{1,0:T(8,128)} %param.23) | copy-start | bytes 49156
  75.6 50.3 %copy-start.9 = (bf16[64,512]{1,0:T(8,128)(2,1)S(1)}, bf16[64,512]{1,0:T(8,128)(2,1)}, u32[]{:S(2)}) copy-start(bf16[64,512]{1,0:T(8,128)(2,1)} %param.20) | copy-start | bytes 196612
  80.9 19.2 %all-to-all-start = ((s32[16,1,6]{2,1,0:T(1,128)}), s32[16,1,6]{2,1,0:T(1,128)S(1)}, u32[]{:S(2)}, u32[]{:S(2)}) async-start(s32[16,1,6]{2,1,0:T(1,128)} %bitcast.2), calls=%async_computation | async-start | bytes 16384 | tf_op jit(solution)/shard_map/all_to_all | solution.py:103
  100.1 13.0 %all-to-all-start.1 = ((f32[16,1,384]{2,1,0:T(1,128)}), f32[16,1,384]{2,1,0:T(1,128)S(1)}, u32[]{:S(2)}, u32[]{:S(2)}) async-start(f32[16,1,384]{2,1,0:T(1,128)} %reshape.84), calls=%async_computation.1 | async-start | bytes 49152 | tf_op jit(solution)/shard_map/all_to_all | solution.py:102
  114.6 12.6 %copy-start.6 = (f32[64,64]{1,0:T(8,128)}, f32[64,64]{1,0:T(8,128)S(1)}, u32[]{:S(2)}) copy-start(f32[64,64]{1,0:T(8,128)S(1)} %fusion.36) | copy-start | bytes 49156
  127.1 8.5 %collective-permute-start.9 = (f32[1,32,64]{2,1,0:T(8,128)S(1)}, f32[1,32,64]{2,1,0:T(8,128)S(1)}, u32[]{:S(2)}, u32[]{:S(2)}) collective-permute-start(f32[1,32,64]{2,1,0:T(8,128)S(1)} %slice.185), channel_id=1, source_target_pairs={{2,0},{4,2},{6,4},{8,6},{10,8},{12,10},{14,12},{16,14},{18,16},{20... | collective-permute-start | bytes 24584 | tf_op jit(solution)/shard_map/ppermute | solution.py:19
  133.2 7.4 %collective-permute-start.8 = (f32[1,32,64]{2,1,0:T(8,128)S(1)}, f32[1,32,64]{2,1,0:T(8,128)S(1)}, u32[]{:S(2)}, u32[]{:S(2)}) collective-permute-start(f32[1,32,64]{2,1,0:T(8,128)S(1)} %slice.181), channel_id=1, source_target_pairs={{0,2},{2,4},{4,6},{6,8},{8,10},{10,12},{12,14},{14,16},{16,18},{18... | collective-permute-start | bytes 24584 | tf_op jit(solution)/shard_map/ppermute | solution.py:16
  (4 other events, 6.1 us)
Sparse Core Ops, SparseCore 0:
  80.3 17.6 all-reduce.1
where the time goes:
time: 150 us
  starting transfers between devices  44.4 us (30%)
  matrix products  29.3 us (20%)
  waiting for transfers between devices  27.6 us (18%)
  between operations  14.8 us (10%)
  other arithmetic  12.8 us (9%)
  local copies, waits for them, and re-layouts  10.9 us (7%)
  blocking collectives  9.95 us (7%)
    ppermute x5, starting transfers between devices, padded_2(): lax.ppermute(lax.slice_in_dim(block, 0, width, axis=dim), axis, backward)  17.6 us
    ppermute x5, starting transfers between devices, padded_2(): lax.ppermute(lax.slice_in_dim(block, block.shape[dim] - width, None, axis...  14.3 us
    psum x1, waiting for transfers between devices, local(): density_term = lax.psum(partial_density, 'orb')  11.5 us
    ppermute x5, waiting for transfers between devices, padded_2(): lax.ppermute(lax.slice_in_dim(block, block.shape[dim] - width, None, axis...  11.3 us
    dot_general x5, matrix products, operator(): jnp.dot(values_bf.reshape(-1, nodes), stiffness, preferred_element_type=j...  10.6 us
    all_to_all x1, blocking collectives, local(): lax.all_to_all(back_values, 'dom', split_axis=0, concat_axis=0, tiled=True)  9.95 us
    dot_general x5, matrix products, assemble_local(): jnp.einsum('ckj,cok->coj', onehot, right_face, precision=lax.Precision.HI...  9.03 us
    dot_general x5, matrix products, assemble_local(): jnp.einsum('ckj,coj->cok', onehot, left_next, precision=lax.Precision.HIG...  7.53 us
  transfers between devices with their start and end apart: 13, of which 6 were waited for; matrix products, arithmetic and copies ran while one was open for 19% of the time, Pallas kernels for 0%

commit v1 on v0

--- a/solution.py
+++ b/solution.py
@@ -6,6 +6,12 @@
 ITERS = 4
 relax = 0.25
 step_rate = 0.1
+
+
+def summed_here(block, mesh_axis):
+    parts = lax.all_gather(block, mesh_axis, axis=0, tiled=False)
+    result = parts.sum(axis=0)
+    return result
 
 
 def padded_2(block, sides, width):
@@ -78,7 +84,7 @@
     adjoint = iterate.astype(jnp.bfloat16)
     partial_density = jnp.sum(orbitals.astype(jnp.float32) * iterate, axis=1)
     restrict_full = restrict.astype(jnp.float32)
-    density_term = lax.psum(partial_density, "orb")
+    density_term = summed_here(partial_density, "orb")
     projected = jnp.dot(density_term, restrict_full, precision=lax.Precision.HIGHEST)
     coarse_cols = projected.shape[1]
     dest_owner = owner[:, 0]

time: 150 us -> 124 us (0.83)
  between operations: 14.8 us -> 1.34 us
  waiting for transfers between devices: 27.6 us -> 17.5 us
  local copies, waits for them, and re-layouts: 10.9 us -> 6.79 us
  blocking collectives: 9.95 us -> 11.9 us
  starting transfers between devices: 44.4 us -> 42.6 us
    psum x1 -> x0, waiting for transfers between devices: 11.5 us -> none  [local(): density_term = lax.psum(partial_density, 'orb')]
    ppermute x5, starting transfers between devices: 17.6 us -> 14.1 us  [padded_2(): lax.ppermute(lax.slice_in_dim(block, 0, width, axis=dim), axis, backward)]
    slice x5, local copies, waits for them, and re-layouts: 5.15 us -> 3.12 us  [assemble_local(): partial_sum[:, :, faces:nodes - faces]]
    all_gather x0 -> x1, blocking collectives: none -> 1.93 us  [summed_here(): parts = lax.all_gather(block, mesh_axis, axis=0, tiled=False)]
    ppermute x5, starting transfers between devices: 14.3 us -> 16 us  [padded_2(): lax.ppermute(lax.slice_in_dim(block, block.shape[dim] - width, None, axis...]
    all_to_all x1, starting transfers between devices: 5.55 us -> 7.22 us  [local(): lax.all_to_all(send_ids, 'dom', split_axis=0, concat_axis=0, tiled=True)]
    all_to_all x1, starting transfers between devices: 6.97 us -> 5.32 us  [local(): lax.all_to_all(send_values, 'dom', split_axis=0, concat_axis=0, tiled=True)]
  transfers between devices with their start and end apart: 13 -> 12, of which waited for: 6 -> 6; matrix products, arithmetic and copies ran while one was open for 19% -> 33% of each run, Pallas kernels for 0% -> 0%
where the time goes in v1:
time: 124 us; the launch traced here: 123 us
  starting transfers between devices  42.6 us (34%)
  matrix products  28.9 us (23%)
  waiting for transfers between devices  17.5 us (14%)
  other arithmetic  14.2 us (11%)
  blocking collectives  11.9 us (10%)
  local copies, waits for them, and re-layouts  6.79 us (5%)
  between operations  1.34 us (1%)
    ppermute x5, starting transfers between devices, padded_2(): lax.ppermute(lax.slice_in_dim(block, block.shape[dim] - width, None, axis...  16 us
    ppermute x5, starting transfers between devices, padded_2(): lax.ppermute(lax.slice_in_dim(block, 0, width, axis=dim), axis, backward)  14.1 us
    ppermute x5, waiting for transfers between devices, padded_2(): lax.ppermute(lax.slice_in_dim(block, block.shape[dim] - width, None, axis...  12.7 us
    dot_general x5, matrix products, operator(): jnp.dot(values_bf.reshape(-1, nodes), stiffness, preferred_element_type=j...  11 us
    all_to_all x1, blocking collectives, local(): lax.all_to_all(back_values, 'dom', split_axis=0, concat_axis=0, tiled=True)  9.95 us
    dot_general x5, matrix products, assemble_local(): jnp.einsum('ckj,cok->coj', onehot, right_face, precision=lax.Precision.HI...  9.03 us
    dot_general x5, matrix products, assemble_local(): jnp.einsum('ckj,coj->cok', onehot, left_next, precision=lax.Precision.HIG...  7.57 us
    all_to_all x1, starting transfers between devices, local(): lax.all_to_all(send_ids, 'dom', split_axis=0, concat_axis=0, tiled=True)  7.22 us
  transfers between devices with their start and end apart: 12, of which 6 were waited for; matrix products, arithmetic and copies ran while one was open for 33% of the time, Pallas kernels for 0%

profile of v1, /device:TPU:8, one launch (start us, length us, event | category | flops | bytes accessed | tf_op | source)
XLA Modules:
  0.0 123.1 jit_solution(17083634524664530923)
XLA Ops:
  3.8 7.2 %all-to-all-start = ((s32[16,1,6]{2,1,0:T(1,128)}), s32[16,1,6]{2,1,0:T(1,128)S(1)}, u32[]{:S(2)}, u32[]{:S(2)}) async-start(s32[16,1,6]{2,1,0:T(1,128)} %bitcast.2), calls=%async_computation | async-start | bytes 16384 | tf_op jit(solution)/shard_map/all_to_all | solution.py:109
  11.1 3.3 %fusion.11 = f32[48,32,512]{2,1,0:T(8,128)S(1)} fusion(bf16[48,32,512]{2,1,0:T(8,128)(2,1)} %param.13, f32[32]{0:T(128)} %param.14, f32[48,512]{1,0:T(8,128)} %param.16, f32[48]{0:T(128)} %param.15, bf16[512,512]{1,0:T(8,128)(2,1)S(1)} %copy-done), kind=kOutput, calls=%fused_computation.22 | convolution fusion | flops 812384256 | bytes 5341504 | tf_op jit(solution)/shard_map/dot_general | solution.py:73
  14.4 4.3 %collective-permute-start.1 = (f32[1,32,64]{2,1,0:T(8,128)S(1)}, f32[1,32,64]{2,1,0:T(8,128)S(1)}, u32[]{:S(2)}, u32[]{:S(2)}) collective-permute-start(f32[1,32,64]{2,1,0:T(8,128)S(1)} %slice.157), channel_id=1, source_target_pairs={{2,0},{4,2},{6,4},{8,6},{10,8},{12,10},{14,12},{16,14},{18,16},{20... | collective-permute-start | bytes 24584 | tf_op jit(solution)/shard_map/ppermute | solution.py:25
  20.5 1.9 %collective-permute-start = (f32[1,32,64]{2,1,0:T(8,128)S(1)}, f32[1,32,64]{2,1,0:T(8,128)S(1)}, u32[]{:S(2)}, u32[]{:S(2)}) collective-permute-start(f32[1,32,64]{2,1,0:T(8,128)S(1)} %slice.153), channel_id=1, source_target_pairs={{0,2},{2,4},{4,6},{6,8},{8,10},{10,12},{12,14},{14,16},{16,18},{18... | collective-permute-start | bytes 24584 | tf_op jit(solution)/shard_map/ppermute | solution.py:22
  24.8 3.1 %collective-permute-done = f32[1,32,64]{2,1,0:T(8,128)S(1)} collective-permute-done((f32[1,32,64]{2,1,0:T(8,128)S(1)}, f32[1,32,64]{2,1,0:T(8,128)S(1)}, u32[]{:S(2)}, u32[]{:S(2)}) %collective-permute-start) | collective-permute-done | bytes 8224 | tf_op jit(solution)/shard_map/ppermute | solution.py:22
  28.1 2.8 %fusion.12 = f32[48,32,512]{2,1,0:T(8,128)S(1)} fusion(f32[32]{0:T(128)S(1)} %copy-done.9, f32[48,512]{1,0:T(8,128)S(1)} %copy-done.5, f32[48]{0:T(128)S(1)} %copy-done.10, f32[48,32,64]{2,1,0:T(8,128)S(1)} %fusion.30, f32[48,32,384]{2,1,0:T(8,128)S(1)} %slice.155, f32[48,32,64]{2,1,0:T(8,128)S(1)} %slice_add_fusion.4, ...), kind=kOutput, calls=%fused_computation.23 | convolution fusion | flops 820248576 | bytes 8487232 | tf_op jit(solution)/shard_map/dot_general | solution.py:73
  30.9 2.6 %collective-permute-start.3 = (f32[1,32,64]{2,1,0:T(8,128)S(1)}, f32[1,32,64]{2,1,0:T(8,128)S(1)}, u32[]{:S(2)}, u32[]{:S(2)}) collective-permute-start(f32[1,32,64]{2,1,0:T(8,128)S(1)} %slice.164), channel_id=1, source_target_pairs={{2,0},{4,2},{6,4},{8,6},{10,8},{12,10},{14,12},{16,14},{18,16},{20... | collective-permute-start | bytes 24584 | tf_op jit(solution)/shard_map/ppermute | solution.py:25
  36.2 3.4 %collective-permute-start.2 = (f32[1,32,64]{2,1,0:T(8,128)S(1)}, f32[1,32,64]{2,1,0:T(8,128)S(1)}, u32[]{:S(2)}, u32[]{:S(2)}) collective-permute-start(f32[1,32,64]{2,1,0:T(8,128)S(1)} %slice.160), channel_id=1, source_target_pairs={{0,2},{2,4},{4,6},{6,8},{8,10},{10,12},{12,14},{14,16},{16,18},{18... | collective-permute-start | bytes 24584 | tf_op jit(solution)/shard_map/ppermute | solution.py:22
  41.1 2.5 %collective-permute-done.2 = f32[1,32,64]{2,1,0:T(8,128)S(1)} collective-permute-done((f32[1,32,64]{2,1,0:T(8,128)S(1)}, f32[1,32,64]{2,1,0:T(8,128)S(1)}, u32[]{:S(2)}, u32[]{:S(2)}) %collective-permute-start.2) | collective-permute-done | bytes 8224 | tf_op jit(solution)/shard_map/ppermute | solution.py:22
  43.8 2.9 %fusion.6 = f32[48,32,512]{2,1,0:T(8,128)S(1)} fusion(bf16[48,32,512]{2,1,0:T(8,128)(2,1)S(1)} %copy-done.1, f32[48,32,64]{2,1,0:T(8,128)S(1)} %fusion.31, f32[48,32,384]{2,1,0:T(8,128)S(1)} %slice.162, f32[48,32,64]{2,1,0:T(8,128)S(1)} %slice_add_fusion.3, f32[48,32,64]{2,1,0:T(8,128)S(1)} %fusion.30, f32[48,32,384]{2,1,0:T(8,128)S(1)} %slice.155, ...), kind=kLoop, calls=%fused_computation.17 | loop fusion | flops 9437184 | bytes 11010048 | tf_op jit(solution)/shard_map/add | solution.py:83
  47.8 1.9 %collective-permute-start.5 = (f32[1,32,64]{2,1,0:T(8,128)S(1)}, f32[1,32,64]{2,1,0:T(8,128)S(1)}, u32[]{:S(2)}, u32[]{:S(2)}) collective-permute-start(f32[1,32,64]{2,1,0:T(8,128)S(1)} %slice.171), channel_id=1, source_target_pairs={{2,0},{4,2},{6,4},{8,6},{10,8},{12,10},{14,12},{16,14},{18,16},{20... | collective-permute-start | bytes 24584 | tf_op jit(solution)/shard_map/ppermute | solution.py:25
  52.4 3.9 %collective-permute-start.4 = (f32[1,32,64]{2,1,0:T(8,128)S(1)}, f32[1,32,64]{2,1,0:T(8,128)S(1)}, u32[]{:S(2)}, u32[]{:S(2)}) collective-permute-start(f32[1,32,64]{2,1,0:T(8,128)S(1)} %slice.167), channel_id=1, source_target_pairs={{0,2},{2,4},{4,6},{6,8},{8,10},{10,12},{12,14},{14,16},{16,18},{18... | collective-permute-start | bytes 24584 | tf_op jit(solution)/shard_map/ppermute | solution.py:22
  57.8 2.0 %collective-permute-done.4 = f32[1,32,64]{2,1,0:T(8,128)S(1)} collective-permute-done((f32[1,32,64]{2,1,0:T(8,128)S(1)}, f32[1,32,64]{2,1,0:T(8,128)S(1)}, u32[]{:S(2)}, u32[]{:S(2)}) %collective-permute-start.4) | collective-permute-done | bytes 8224 | tf_op jit(solution)/shard_map/ppermute | solution.py:22
  60.0 2.7 %fusion.14 = f32[48,32,512]{2,1,0:T(8,128)S(1)} fusion(f32[32]{0:T(128)S(1)} %copy-done.9, f32[48,512]{1,0:T(8,128)S(1)} %copy-done.5, f32[48]{0:T(128)S(1)} %copy-done.10, bf16[512,512]{1,0:T(8,128)(2,1)S(1)} %copy-done, f32[48,32,512]{2,1,0:T(8,128)S(1)} %fusion.6, f32[48,32,64]{2,1,0:T(8,128)S(1)} %fusion.32, f32[48,32,384]{2,1,0:T(8,128)S(1)} %slice.169, ...), kind=kOutput, calls=%fused_computation.25 | convolution fusion | flops 818675712 | bytes 11632960 | tf_op jit(solution)/shard_map/dot_general | solution.py:73
  67.4 4.3 %collective-permute-start.6 = (f32[1,32,64]{2,1,0:T(8,128)S(1)}, f32[1,32,64]{2,1,0:T(8,128)S(1)}, u32[]{:S(2)}, u32[]{:S(2)}) collective-permute-start(f32[1,32,64]{2,1,0:T(8,128)S(1)} %slice.174), channel_id=1, source_target_pairs={{0,2},{2,4},{4,6},{6,8},{8,10},{10,12},{12,14},{14,16},{16,18},{18... | collective-permute-start | bytes 24584 | tf_op jit(solution)/shard_map/ppermute | solution.py:22
  75.1 3.9 %fusion.2 = (f32[48,512]{1,0:T(8,128)S(1)}, bf16[48,32,512]{2,1,0:T(8,128)(2,1)}) fusion(bf16[48,32,512]{2,1,0:T(8,128)(2,1)S(1)} %copy-done.3, f32[48,32,64]{2,1,0:T(8,128)S(1)} %fusion.33, f32[48,32,384]{2,1,0:T(8,128)S(1)} %slice.176, f32[48,32,64]{2,1,0:T(8,128)S(1)} %slice_add_fusion.1, f32[48,32,512]{2,1,0:T(8,128)S(1)} %fusion.6, ...), kind=kLoop, calls=%fused_computation.13 | loop fusion | flops 11771904 | bytes 14254080 | tf_op jit(solution)/shard_map/reduce_sum | solution.py:85
  79.0 1.9 %all-gather = f32[96,512]{1,0:T(8,128)S(1)} all-gather(f32[48,512]{1,0:T(8,128)S(1)} %get-tuple-element.3), channel_id=2, replica_groups=mesh['dom'=16,'orb'=2] {'orb'}, dimensions={0}, use_global_device_ids=true | all-gather | bytes 294912 | tf_op jit(solution)/shard_map/all_gather | solution.py:12
  82.2 5.3 %all-to-all-start.1 = ((f32[16,1,384]{2,1,0:T(1,128)}), f32[16,1,384]{2,1,0:T(1,128)S(1)}, u32[]{:S(2)}, u32[]{:S(2)}) async-start(f32[16,1,384]{2,1,0:T(1,128)} %reshape.85), calls=%async_computation.1 | async-start | bytes 49152 | tf_op jit(solution)/shard_map/all_to_all | solution.py:108
  88.8 4.8 %all-to-all-done.1 = f32[16,1,384]{2,1,0:T(1,128)S(1)} async-done(((f32[16,1,384]{2,1,0:T(1,128)}), f32[16,1,384]{2,1,0:T(1,128)S(1)}, u32[]{:S(2)}, u32[]{:S(2)}) %all-to-all-start.1) | async-done | bytes 24608 | tf_op jit(solution)/shard_map/all_to_all | solution.py:108
  95.4 9.9 %all_to_all.16 = f32[16,1,384]{2,1,0:T(1,128)S(1)} all-to-all(f32[16,1,384]{2,1,0:T(1,128)S(1)} %reshape.87), channel_id=1, replica_groups=mesh['dom'=16,'orb'=2] {'dom'}, dimensions={0} | all-to-all | bytes 49152 | tf_op jit(solution)/shard_map/all_to_all | solution.py:121
  107.6 3.4 %collective-permute-start.9 = (f32[1,32,64]{2,1,0:T(8,128)S(1)}, f32[1,32,64]{2,1,0:T(8,128)S(1)}, u32[]{:S(2)}, u32[]{:S(2)}) collective-permute-start(f32[1,32,64]{2,1,0:T(8,128)S(1)} %slice.185), channel_id=1, source_target_pairs={{2,0},{4,2},{6,4},{8,6},{10,8},{12,10},{14,12},{16,14},{18,16},{20... | collective-permute-start | bytes 24584 | tf_op jit(solution)/shard_map/ppermute | solution.py:25
  113.4 2.5 %collective-permute-start.8 = (f32[1,32,64]{2,1,0:T(8,128)S(1)}, f32[1,32,64]{2,1,0:T(8,128)S(1)}, u32[]{:S(2)}, u32[]{:S(2)}) collective-permute-start(f32[1,32,64]{2,1,0:T(8,128)S(1)} %slice.181), channel_id=1, source_target_pairs={{0,2},{2,4},{4,6},{6,8},{8,10},{10,12},{12,14},{14,16},{16,18},{18... | collective-permute-start | bytes 24584 | tf_op jit(solution)/shard_map/ppermute | solution.py:22
  117.7 3.2 %collective-permute-done.8 = f32[1,32,64]{2,1,0:T(8,128)S(1)} collective-permute-done((f32[1,32,64]{2,1,0:T(8,128)S(1)}, f32[1,32,64]{2,1,0:T(8,128)S(1)}, u32[]{:S(2)}, u32[]{:S(2)}) %collective-permute-start.8) | collective-permute-done | bytes 8224 | tf_op jit(solution)/shard_map/ppermute | solution.py:22
  121.0 2.1 %pad_maximum_fusion = bf16[48,32,512]{2,1,0:T(8,128)(2,1)} fusion(bf16[48,32,64]{2,1,0:T(8,128)(2,1)S(1)} %fusion.35, bf16[48,32,384]{2,1,0:T(8,128)(2,1)S(1)} %slice.209, bf16[48,32,64]{2,1,0:T(8,128)(2,1)S(1)} %fusion.38), kind=kLoop, calls=%fused_computation.27 | loop fusion | flops 4718592 | bytes 3145728 | tf_op jit(solution)/shard_map/concatenate | solution.py:63
  (100 shorter events, 35.9 us)
Async XLA Ops:
  0.6 10.4 %copy-start = (bf16[512,512]{1,0:T(8,128)(2,1)S(1)}, bf16[512,512]{1,0:T(8,128)(2,1)}, u32[]{:S(2)}) copy-start(bf16[512,512]{1,0:T(8,128)(2,1)} %param.17) | copy-start | bytes 1572868
  3.8 78.4 %all-to-all-start = ((s32[16,1,6]{2,1,0:T(1,128)}), s32[16,1,6]{2,1,0:T(1,128)S(1)}, u32[]{:S(2)}, u32[]{:S(2)}) async-start(s32[16,1,6]{2,1,0:T(1,128)} %bitcast.2), calls=%async_computation | async-start | bytes 16384 | tf_op jit(solution)/shard_map/all_to_all | solution.py:109
  11.1 7.6 %copy-start.2 = (s32[48,64]{1,0:T(8,128)S(1)}, s32[48,64]{1,0:T(8,128)}, u32[]{:S(2)}) copy-start(s32[48,64]{1,0:T(8,128)} %param.18) | copy-start | bytes 36868
  14.4 8.9 %collective-permute-start.1 = (f32[1,32,64]{2,1,0:T(8,128)S(1)}, f32[1,32,64]{2,1,0:T(8,128)S(1)}, u32[]{:S(2)}, u32[]{:S(2)}) collective-permute-start(f32[1,32,64]{2,1,0:T(8,128)S(1)} %slice.157), channel_id=1, source_target_pairs={{2,0},{4,2},{6,4},{8,6},{10,8},{12,10},{14,12},{16,14},{18,16},{20... | collective-permute-start | bytes 24584 | tf_op jit(solution)/shard_map/ppermute | solution.py:25
  20.5 7.4 %collective-permute-start = (f32[1,32,64]{2,1,0:T(8,128)S(1)}, f32[1,32,64]{2,1,0:T(8,128)S(1)}, u32[]{:S(2)}, u32[]{:S(2)}) collective-permute-start(f32[1,32,64]{2,1,0:T(8,128)S(1)} %slice.153), channel_id=1, source_target_pairs={{0,2},{2,4},{4,6},{6,8},{8,10},{10,12},{12,14},{14,16},{16,18},{18... | collective-permute-start | bytes 24584 | tf_op jit(solution)/shard_map/ppermute | solution.py:22
  23.3 4.8 %copy-start.1 = (bf16[48,32,512]{2,1,0:T(8,128)(2,1)S(1)}, bf16[48,32,512]{2,1,0:T(8,128)(2,1)}, u32[]{:S(2)}) copy-start(bf16[48,32,512]{2,1,0:T(8,128)(2,1)} %param.13) | copy-start | bytes 4718596
  23.3 4.8 %copy-start.5 = (f32[48,512]{1,0:T(8,128)S(1)}, f32[48,512]{1,0:T(8,128)}, u32[]{:S(2)}) copy-start(f32[48,512]{1,0:T(8,128)} %param.16) | copy-start | bytes 294916
  23.3 4.8 %copy-start.9 = (f32[32]{0:T(128)S(1)}, f32[32]{0:T(128)}, u32[]{:S(2)}) copy-start(f32[32]{0:T(128)} %param.14) | copy-start | bytes 388
  23.3 4.8 %copy-start.10 = (f32[48]{0:T(128)S(1)}, f32[48]{0:T(128)}, u32[]{:S(2)}) copy-start(f32[48]{0:T(128)} %param.15) | copy-start | bytes 580
  30.9 8.7 %collective-permute-start.3 = (f32[1,32,64]{2,1,0:T(8,128)S(1)}, f32[1,32,64]{2,1,0:T(8,128)S(1)}, u32[]{:S(2)}, u32[]{:S(2)}) collective-permute-start(f32[1,32,64]{2,1,0:T(8,128)S(1)} %slice.164), channel_id=1, source_target_pairs={{2,0},{4,2},{6,4},{8,6},{10,8},{12,10},{14,12},{16,14},{18,16},{20... | collective-permute-start | bytes 24584 | tf_op jit(solution)/shard_map/ppermute | solution.py:25
  36.2 7.4 %collective-permute-start.2 = (f32[1,32,64]{2,1,0:T(8,128)S(1)}, f32[1,32,64]{2,1,0:T(8,128)S(1)}, u32[]{:S(2)}, u32[]{:S(2)}) collective-permute-start(f32[1,32,64]{2,1,0:T(8,128)S(1)} %slice.160), channel_id=1, source_target_pairs={{0,2},{2,4},{4,6},{6,8},{8,10},{10,12},{12,14},{14,16},{16,18},{18... | collective-permute-start | bytes 24584 | tf_op jit(solution)/shard_map/ppermute | solution.py:22
  47.8 8.5 %collective-permute-start.5 = (f32[1,32,64]{2,1,0:T(8,128)S(1)}, f32[1,32,64]{2,1,0:T(8,128)S(1)}, u32[]{:S(2)}, u32[]{:S(2)}) collective-permute-start(f32[1,32,64]{2,1,0:T(8,128)S(1)} %slice.171), channel_id=1, source_target_pairs={{2,0},{4,2},{6,4},{8,6},{10,8},{12,10},{14,12},{16,14},{18,16},{20... | collective-permute-start | bytes 24584 | tf_op jit(solution)/shard_map/ppermute | solution.py:25
  52.4 7.4 %collective-permute-start.4 = (f32[1,32,64]{2,1,0:T(8,128)S(1)}, f32[1,32,64]{2,1,0:T(8,128)S(1)}, u32[]{:S(2)}, u32[]{:S(2)}) collective-permute-start(f32[1,32,64]{2,1,0:T(8,128)S(1)} %slice.167), channel_id=1, source_target_pairs={{0,2},{2,4},{4,6},{6,8},{8,10},{10,12},{12,14},{14,16},{16,18},{18... | collective-permute-start | bytes 24584 | tf_op jit(solution)/shard_map/ppermute | solution.py:22
  62.8 8.9 %collective-permute-start.7 = (f32[1,32,64]{2,1,0:T(8,128)S(1)}, f32[1,32,64]{2,1,0:T(8,128)S(1)}, u32[]{:S(2)}, u32[]{:S(2)}) collective-permute-start(f32[1,32,64]{2,1,0:T(8,128)S(1)} %slice.178), channel_id=1, source_target_pairs={{2,0},{4,2},{6,4},{8,6},{10,8},{12,10},{14,12},{16,14},{18,16},{20... | collective-permute-start | bytes 24584 | tf_op jit(solution)/shard_map/ppermute | solution.py:25
  67.4 7.7 %copy-start.3 = (bf16[48,32,512]{2,1,0:T(8,128)(2,1)S(1)}, bf16[48,32,512]{2,1,0:T(8,128)(2,1)}, u32[]{:S(2)}) copy-start(bf16[48,32,512]{2,1,0:T(8,128)(2,1)} %param.12) | copy-start | bytes 4718596
  67.4 7.6 %collective-permute-start.6 = (f32[1,32,64]{2,1,0:T(8,128)S(1)}, f32[1,32,64]{2,1,0:T(8,128)S(1)}, u32[]{:S(2)}, u32[]{:S(2)}) collective-permute-start(f32[1,32,64]{2,1,0:T(8,128)S(1)} %slice.174), channel_id=1, source_target_pairs={{0,2},{2,4},{4,6},{6,8},{8,10},{10,12},{12,14},{14,16},{16,18},{18... | collective-permute-start | bytes 24584 | tf_op jit(solution)/shard_map/ppermute | solution.py:22
  75.1 5.9 %copy-start.6 = (bf16[512,64]{0,1:T(8,128)(2,1)S(1)}, bf16[512,64]{0,1:T(8,128)(2,1)}, u32[]{:S(2)}) copy-start(bf16[512,64]{0,1:T(8,128)(2,1)} %param.19) | copy-start | bytes 196612
  75.1 19.8 %copy-start.8 = (f32[64,64]{1,0:T(8,128)S(1)}, f32[64,64]{1,0:T(8,128)}, u32[]{:S(2)}) copy-start(f32[64,64]{1,0:T(8,128)} %param.23) | copy-start | bytes 49156
  75.1 31.2 %copy-start.7 = (bf16[64,512]{1,0:T(8,128)(2,1)S(1)}, bf16[64,512]{1,0:T(8,128)(2,1)}, u32[]{:S(2)}) copy-start(bf16[64,512]{1,0:T(8,128)(2,1)} %param.20) | copy-start | bytes 196612
  82.2 11.4 %all-to-all-start.1 = ((f32[16,1,384]{2,1,0:T(1,128)}), f32[16,1,384]{2,1,0:T(1,128)S(1)}, u32[]{:S(2)}, u32[]{:S(2)}) async-start(f32[16,1,384]{2,1,0:T(1,128)} %reshape.85), calls=%async_computation.1 | async-start | bytes 49152 | tf_op jit(solution)/shard_map/all_to_all | solution.py:108
  95.0 12.6 %copy-start.4 = (f32[64,64]{1,0:T(8,128)}, f32[64,64]{1,0:T(8,128)S(1)}, u32[]{:S(2)}) copy-start(f32[64,64]{1,0:T(8,128)S(1)} %fusion.36) | copy-start | bytes 49156
  107.6 8.3 %collective-permute-start.9 = (f32[1,32,64]{2,1,0:T(8,128)S(1)}, f32[1,32,64]{2,1,0:T(8,128)S(1)}, u32[]{:S(2)}, u32[]{:S(2)}) collective-permute-start(f32[1,32,64]{2,1,0:T(8,128)S(1)} %slice.185), channel_id=1, source_target_pairs={{2,0},{4,2},{6,4},{8,6},{10,8},{12,10},{14,12},{16,14},{18,16},{20... | collective-permute-start | bytes 24584 | tf_op jit(solution)/shard_map/ppermute | solution.py:25
  113.4 7.4 %collective-permute-start.8 = (f32[1,32,64]{2,1,0:T(8,128)S(1)}, f32[1,32,64]{2,1,0:T(8,128)S(1)}, u32[]{:S(2)}, u32[]{:S(2)}) collective-permute-start(f32[1,32,64]{2,1,0:T(8,128)S(1)} %slice.181), channel_id=1, source_target_pairs={{0,2},{2,4},{4,6},{6,8},{8,10},{10,12},{12,14},{14,16},{16,18},{18... | collective-permute-start | bytes 24584 | tf_op jit(solution)/shard_map/ppermute | solution.py:22
